TPU v7x, 512 devices: a whole 4x8x8 slice. The times are simulated.
512 devices in a mesh: row: 16 (over z, y_hi), col: 32 (over x, y_lo, core).
Axes of the slice: x: 4, y: 8 (y_hi: 2, y_lo: 4; y = y_hi * 4 + y_lo), z: 8, core: 2. Of those that a mesh axis runs over, the one named last changes fastest.
Arguments:
- scalars: float32 [1, 256, 256, 512], P(None, 'row', 'col'), may hold values from -6 to 6
- velocity: bfloat16 [3, 256, 256, 512], P(None, 'row', 'col'), may hold values from -6 to 6
- first_x: bfloat16 [512, 512], replicated, may hold values from -0.25 to 0.25
- second_x: bfloat16 [512, 512], replicated, may hold values from -0.25 to 0.25
- first_y: bfloat16 [256, 256], replicated, may hold values from -0.375 to 0.375
- second_y: bfloat16 [256, 256], replicated, may hold values from -0.375 to 0.375
- first_z: bfloat16 [256, 256], replicated, may hold values from -0.375 to 0.375
- second_z: bfloat16 [256, 256], replicated, may hold values from -0.375 to 0.375
Outputs:
- updated: float32 [1, 256, 256, 512], P(None, 'row', 'col')
All inputs are finite; a program needn't handle non-finite values.
Results may differ from a plain program's by a relative error of at most 0.0021.
Values may be sent and summed in bfloat16 or wider, within the bound.
No kernel may reach another device: no remote copies, remote signals or barrier semaphores. Data moves between devices by JAX's collectives and lax.ppermute only.
A program may use at most 64 MiB of HBM per device.

v0:
```python
import jax
import jax.numpy as jnp
from jax import lax
from jax.sharding import PartitionSpec as P

diffusion_coefficient = 0.5
step_weight = 0.5


def contract_last(scalar_values, matrix):
    return lax.dot_general(
        scalar_values,
        matrix,
        (((scalar_values.ndim - 1,), (1,)), ((), ())),
        preferred_element_type=jnp.float32,
    )


def contract_middle(scalar_values, matrix):
    return jnp.einsum("syc,ky->skc", scalar_values, matrix, preferred_element_type=jnp.float32)


def contract_z(scalar_values, matrix):
    blocks = scalar_values.shape[2]
    depth_z = scalar_values.shape[4]
    shaped = matrix.reshape(matrix.shape[0] // depth_z, depth_z, blocks, depth_z)
    return jnp.einsum(
        "sajxz,JZjz->saJxZ", scalar_values, shaped, preferred_element_type=jnp.float32
    )


def derivative_pair(scalar_values, first_derivative_matrix, second_derivative_matrix, apply_matrix):
    return (
        apply_matrix(scalar_values, first_derivative_matrix),
        apply_matrix(scalar_values, second_derivative_matrix),
    )


def axis_contribution(
    scalar_values, velocity_field, first_derivative_matrix, second_derivative_matrix, apply_matrix
):
    velocity_flux = velocity_field.astype(jnp.float32)
    flux_product = (velocity_flux * scalar_values.astype(jnp.float32)).astype(jnp.bfloat16)
    scalar_gradient, second_derivative = derivative_pair(
        scalar_values, first_derivative_matrix, second_derivative_matrix, apply_matrix
    )
    advected_scalar = apply_matrix(flux_product, first_derivative_matrix)
    return (
        -0.5 * (velocity_flux * scalar_gradient + advected_scalar)
        + diffusion_coefficient * second_derivative
    )


def body(scalars, velocity, first_x, second_x, first_y, second_y, first_z, second_z):
    scalar_count = scalars.shape[0]
    rows_local = scalars.shape[1]
    depth_z = scalars.shape[2]
    length_x = scalars.shape[3]
    compiled_step = scalars.astype(jnp.bfloat16)
    x_term = axis_contribution(compiled_step, velocity[0], first_x, second_x, contract_last)
    outgoing = jnp.concatenate([compiled_step, velocity[1:]], axis=0)
    outgoing = jnp.transpose(outgoing, (0, 1, 3, 2)).reshape(
        scalar_count + 2, rows_local, length_x * depth_z
    )
    pencil_y = lax.all_to_all(outgoing, "row", split_axis=2, concat_axis=1, tiled=True)
    y_term = axis_contribution(
        pencil_y[:scalar_count], pencil_y[scalar_count], first_y, second_y, contract_middle
    )
    onward = jnp.concatenate([pencil_y[:scalar_count], pencil_y[scalar_count + 1 :]], axis=0)
    pencil_z = lax.all_to_all(onward, "col", split_axis=1, concat_axis=2, tiled=True)
    blocks = lax.axis_size("col")
    width_y = pencil_z.shape[1]
    columns = pencil_y.shape[2]
    pencil_z = pencil_z.reshape(scalar_count + 1, width_y, blocks, columns // depth_z, depth_z)
    z_term = axis_contribution(
        pencil_z[:scalar_count], pencil_z[scalar_count], first_z, second_z, contract_z
    )
    z_term = z_term.reshape(scalar_count, width_y, blocks * columns)
    z_lines = lax.all_to_all(z_term, "col", split_axis=2, concat_axis=1, tiled=True)
    y_back_part, z_back_part = (
        lax.all_to_all(y_term, "row", split_axis=1, concat_axis=2, tiled=True),
        lax.all_to_all(z_lines, "row", split_axis=1, concat_axis=2, tiled=True),
    )
    returned = y_back_part + z_back_part
    returned = returned.reshape(scalar_count, rows_local, length_x, depth_z)
    returned = jnp.transpose(returned, (0, 1, 3, 2))
    return scalars + step_weight * (x_term + returned)


def solution(mesh):
    return jax.shard_map(
        body,
        mesh=mesh,
        in_specs=(
            P(None, "row", "col", None),
            P(None, "row", "col", None),
            P(),
            P(),
            P(),
            P(),
            P(),
            P(),
        ),
        out_specs=P(None, "row", "col", None),
        check_vma=False,
    )
```

profile of v0, /device:TPU:8, one launch (start us, length us, event | category | flops | bytes accessed | tf_op | source)
XLA Modules:
  0.0 201.4 jit_solution(11211925408046868918)
XLA Ops:
  0.0 1.0 convert_element_type.74
  1.0 1.0 slice.32
  2.1 3.4 %copy.35 = bf16[3,16,512,8]{1,3,2,0:T(8,128)(2,1)} copy(bf16[3,16,512,8]{2,3,1,0:T(8,128)(2,1)S(1)} %maximum_bitcast_fusion) | data formatting | bytes 786432 | tf_op jit(solution)/shard_map/transpose | solution.py:62
  5.5 6.8 %copy.95 = bf16[3,16,4096]{1,0,2:T(4,128)(2,1)} copy(bf16[3,16,4096]{1,2,0:T(8,128)(2,1)} %bitcast.143) | data formatting | bytes 786432 | tf_op jit(solution)/shard_map/reshape | solution.py:62
  12.3 6.6 %reshape.147 = bf16[16,2,6144]{2,1,0:T(2,128)(2,1)S(1)} reshape(bf16[4096,3,16]{2,1,0:T(4,128)(2,1)} %bitcast.140) | data formatting | bytes 786432
  18.9 33.6 %all_to_all.66 = bf16[16,2,6144]{2,1,0:T(2,128)(2,1)S(1)} all-to-all(bf16[16,2,6144]{2,1,0:T(2,128)(2,1)S(1)} %reshape.147), channel_id=1, replica_groups=mesh['row'=16,'col'=32] {'row'}, dimensions={0} | all-to-all | bytes 786432 | tf_op jit(solution)/shard_map/all_to_all | solution.py:65
  52.5 5.6 %reshape.148 = bf16[4096,3,16]{2,1,0:T(4,128)(2,1)} reshape(bf16[16,2,6144]{2,1,0:T(2,128)(2,1)S(1)} %all_to_all.66) | data formatting | bytes 786432
  58.1 4.2 %copy.71 = bf16[3,16,16,256]{3,2,1,0:T(8,128)(2,1)S(1)} copy(bf16[3,16,16,256]{1,0,3,2:T(4,128)(2,1)} %bitcast.141) | data formatting | bytes 786432 | tf_op jit(solution)/shard_map/all_to_all | solution.py:65
  62.5 1.0 copy.44
  63.5 5.9 %all-to-all-start.2 = ((bf16[2,256,256]{2,0,1:T(2,128)(2,1)}), bf16[2,256,256]{2,0,1:T(2,128)(2,1)S(1)}, u32[]{:S(2)}, u32[]{:S(2)}) async-start(bf16[2,256,256]{2,0,1:T(2,128)(2,1)} %copy.44), calls=%async_computation.2 | async-start | bytes 524288 | tf_op jit(solution)/shard_map/all_to_all | solution.py:70
  69.4 2.5 %reshape.130 = bf16[32,8,32,8]{3,2,1,0:T(8,128)(2,1)S(1)} reshape(bf16[256,256]{1,0:T(8,128)(2,1)S(1)} %copy-done.6) | data formatting | bytes 262144 | tf_op jit(solution)/shard_map/reshape | solution.py:26
  71.9 1.9 copy.49
  73.8 3.4 %reshape.131 = bf16[32,8,32,8]{3,2,1,0:T(8,128)(2,1)S(1)} reshape(bf16[256,256]{1,0:T(8,128)(2,1)} %param.15) | data formatting | bytes 262144 | tf_op jit(solution)/shard_map/reshape | solution.py:26
  77.2 1.9 copy.55
  79.5 1.0 copy.47
  80.9 1.0 copy.51
  81.9 2.0 fusion.1
  83.9 2.0 fusion.5
  86.6 4.3 %copy.78 = f32[1,8,32,32,8]{1,4,3,2,0:T(8,128)} copy(f32[1,8,32,32,8]{2,3,4,1,0:T(8,128)S(1)} %fusion.4) | data formatting | bytes 524288 | tf_op jit(solution)/shard_map/reshape | solution.py:78
  91.5 38.4 %reduce = f32[8192,8]{1,0:T(8,128)} reduce(f32[8192,1,8]{2,1,0:T(1,128)} %bitcast.139, f32[]{:T(128)} %broadcast.21), dimensions={1}, to_apply=%bitcast.128.reduce_sub_computation | reduce | bytes 524292
  130.0 4.5 %reshape.149 = f32[32,1,2048]{2,1,0:T(1,128)} reshape(f32[8192,8]{1,0:T(8,128)} %reduce) | data formatting | bytes 524288
  134.5 7.7 %all-to-all-start.3 = ((f32[32,1,2048]{2,1,0:T(1,128)}), f32[32,1,2048]{2,1,0:T(1,128)S(1)}, u32[]{:S(2)}, u32[]{:S(2)}) async-start(f32[32,1,2048]{2,1,0:T(1,128)} %reshape.149), calls=%async_computation.3 | async-start | bytes 524288 | tf_op jit(solution)/shard_map/all_to_all | solution.py:79
  143.8 7.7 %all-to-all-done.3 = f32[32,1,2048]{2,1,0:T(1,128)S(1)} async-done(((f32[32,1,2048]{2,1,0:T(1,128)}), f32[32,1,2048]{2,1,0:T(1,128)S(1)}, u32[]{:S(2)}, u32[]{:S(2)}) %all-to-all-start.3) | async-done | bytes 262176 | tf_op jit(solution)/shard_map/all_to_all | solution.py:79
  151.5 4.2 %all-to-all-start.1 = ((f32[1,256,256]{2,0,1:T(1,128)}), f32[1,256,256]{2,0,1:T(1,128)S(1)}, u32[]{:S(2)}, u32[]{:S(2)}) async-start(f32[1,256,256]{2,0,1:T(1,128)} %copy.41), calls=%async_computation.1 | async-start | bytes 524288 | tf_op jit(solution)/shard_map/all_to_all | solution.py:81
  155.7 1.3 reduce.1
  157.0 8.4 %reshape.150 = f32[8192,1,8]{2,1,0:T(1,128)} reshape(f32[32,2048]{1,0:T(8,128)S(1)} %reduce.1) | data formatting | bytes 524288
  165.4 2.8 %copy.79 = f32[1,8,32,256]{3,2,1,0:T(8,128)S(1)} copy(f32[1,8,32,256]{1,3,2,0:T(8,128)} %bitcast.142) | data formatting | bytes 524288 | tf_op jit(solution)/shard_map/all_to_all | solution.py:79
  168.4 1.0 copy.60
  169.4 2.9 %all-to-all-done.1 = f32[1,256,256]{2,0,1:T(1,128)S(1)} async-done(((f32[1,256,256]{2,0,1:T(1,128)}), f32[1,256,256]{2,0,1:T(1,128)S(1)}, u32[]{:S(2)}, u32[]{:S(2)}) %all-to-all-start.1) | async-done | bytes 262176 | tf_op jit(solution)/shard_map/all_to_all | solution.py:81
  172.3 9.2 %all-to-all-start.4 = ((f32[1,256,256]{2,0,1:T(1,128)}), f32[1,256,256]{2,0,1:T(1,128)S(1)}, u32[]{:S(2)}, u32[]{:S(2)}) async-start(f32[1,256,256]{2,0,1:T(1,128)} %copy.60), calls=%async_computation.4 | async-start | bytes 524288 | tf_op jit(solution)/shard_map/all_to_all | solution.py:82
  182.2 15.7 %all-to-all-done.4 = f32[1,256,256]{2,0,1:T(1,128)S(1)} async-done(((f32[1,256,256]{2,0,1:T(1,128)}), f32[1,256,256]{2,0,1:T(1,128)S(1)}, u32[]{:S(2)}, u32[]{:S(2)}) %all-to-all-start.4) | async-done | bytes 262176 | tf_op jit(solution)/shard_map/all_to_all | solution.py:82
  199.3 2.1 %fusion.17 = f32[1,16,8,512]{3,2,1,0:T(8,128)} fusion(f32[1,16,8,512]{3,2,1,0:T(8,128)S(1)} %copy-done.1, f32[16,8,512]{2,1,0:T(8,128)S(1)} %fusion.9, bf16[512,512]{1,0:T(8,128)(2,1)} %param.11, f32[1,16,512,8]{2,3,1,0:T(8,128)S(1)} %copy.64, bf16[1,16,8,512]{3,2,1,0:T(8,128)(2,1)S(1)} %convert_element_type.74), kind=kOutput, calls=%fused_computation.26 | convolution fusion | flops 67436544 | bytes 1703936 | tf_op jit(solution)/shard_map/dot_general | solution.py:11
  (40 shorter events, 6.0 us)
Async XLA Ops:
  0.0 181.5 %copy-start = (bf16[512,512]{1,0:T(8,128)(2,1)S(1)}, bf16[512,512]{1,0:T(8,128)(2,1)}, u32[]{:S(2)}) copy-start(bf16[512,512]{1,0:T(8,128)(2,1)} %param.10) | copy-start | bytes 1572868
  58.1 11.3 %copy-start.6 = (bf16[256,256]{1,0:T(8,128)(2,1)S(1)}, bf16[256,256]{1,0:T(8,128)(2,1)}, u32[]{:S(2)}) copy-start(bf16[256,256]{1,0:T(8,128)(2,1)} %param.14) | copy-start | bytes 393220
  63.5 15.9 %all-to-all-start.2 = ((bf16[2,256,256]{2,0,1:T(2,128)(2,1)}), bf16[2,256,256]{2,0,1:T(2,128)(2,1)S(1)}, u32[]{:S(2)}, u32[]{:S(2)}) async-start(bf16[2,256,256]{2,0,1:T(2,128)(2,1)} %copy.44), calls=%async_computation.2 | async-start | bytes 524288 | tf_op jit(solution)/shard_map/all_to_all | solution.py:70
  80.5 5.4 %copy-start.3 = (bf16[32,8,32,8]{2,0,3,1:T(8,128)(2,1)S(1)}, bf16[32,8,32,8]{2,0,3,1:T(8,128)(2,1)}, u32[]{:S(2)}) copy-start(bf16[32,8,32,8]{2,0,3,1:T(8,128)(2,1)} %copy.49) | copy-start | bytes 393220
  81.9 4.0 %copy-start.4 = (bf16[1,8,32,256]{2,3,1,0:T(8,128)(2,1)S(1)}, bf16[1,8,32,256]{2,3,1,0:T(8,128)(2,1)}, u32[]{:S(2)}) copy-start(bf16[1,8,32,256]{2,3,1,0:T(8,128)(2,1)} %copy.51) | copy-start | bytes 393220
  130.0 12.2 %copy-start.5 = (bf16[256,256]{1,0:T(8,128)(2,1)S(1)}, bf16[256,256]{1,0:T(8,128)(2,1)}, u32[]{:S(2)}) copy-start(bf16[256,256]{1,0:T(8,128)(2,1)} %param.12) | copy-start | bytes 393220
  130.0 12.7 %copy-start.7 = (bf16[256,256]{1,0:T(8,128)(2,1)S(1)}, bf16[256,256]{1,0:T(8,128)(2,1)}, u32[]{:S(2)}) copy-start(bf16[256,256]{1,0:T(8,128)(2,1)} %param.13) | copy-start | bytes 393220
  134.5 17.0 %all-to-all-start.3 = ((f32[32,1,2048]{2,1,0:T(1,128)}), f32[32,1,2048]{2,1,0:T(1,128)S(1)}, u32[]{:S(2)}, u32[]{:S(2)}) async-start(f32[32,1,2048]{2,1,0:T(1,128)} %reshape.149), calls=%async_computation.3 | async-start | bytes 524288 | tf_op jit(solution)/shard_map/all_to_all | solution.py:79
  151.5 20.8 %all-to-all-start.1 = ((f32[1,256,256]{2,0,1:T(1,128)}), f32[1,256,256]{2,0,1:T(1,128)S(1)}, u32[]{:S(2)}, u32[]{:S(2)}) async-start(f32[1,256,256]{2,0,1:T(1,128)} %copy.41), calls=%async_computation.1 | async-start | bytes 524288 | tf_op jit(solution)/shard_map/all_to_all | solution.py:81
  157.0 24.5 %copy-start.2 = (bf16[3,16,8,512]{3,2,1,0:T(8,128)(2,1)S(1)}, bf16[3,16,8,512]{3,2,1,0:T(8,128)(2,1)}, u32[]{:S(2)}) copy-start(bf16[3,16,8,512]{3,2,1,0:T(8,128)(2,1)} %param.9) | copy-start | bytes 1179652
  169.4 30.0 %copy-start.1 = (f32[1,16,8,512]{3,2,1,0:T(8,128)S(1)}, f32[1,16,8,512]{3,2,1,0:T(8,128)}, u32[]{:S(2)}) copy-start(f32[1,16,8,512]{3,2,1,0:T(8,128)} %param.8) | copy-start | bytes 786436
  172.3 25.6 %all-to-all-start.4 = ((f32[1,256,256]{2,0,1:T(1,128)}), f32[1,256,256]{2,0,1:T(1,128)S(1)}, u32[]{:S(2)}, u32[]{:S(2)}) async-start(f32[1,256,256]{2,0,1:T(1,128)} %copy.60), calls=%async_computation.4 | async-start | bytes 524288 | tf_op jit(solution)/shard_map/all_to_all | solution.py:82
where the time goes:
time: 202 us; the launch traced here: 201 us
  local copies, waits for them, and re-layouts  65 us (32%)
  other arithmetic  41 us (20%)
  blocking collectives  33.6 us (17%)
  starting transfers between devices  27 us (13%)
  waiting for transfers between devices  26.4 us (13%)
  matrix products  8.05 us (4%)
    unnamed x1, other arithmetic  38.4 us
    all_to_all x1, blocking collectives, body(): lax.all_to_all(outgoing, 'row', split_axis=2, concat_axis=1, tiled=True)  33.6 us
    unnamed x21, local copies, waits for them, and re-layouts  25.8 us
    all_to_all x1, waiting for transfers between devices, body(): lax.all_to_all(z_lines, 'row', split_axis=1, concat_axis=2, tiled=True)  15.7 us
    reshape x4, local copies, waits for them, and re-layouts, contract_z(): matrix.reshape(matrix.shape[0] // depth_z, depth_z, blocks, depth_z)  9.6 us
    all_to_all x1, starting transfers between devices, body(): lax.all_to_all(z_lines, 'row', split_axis=1, concat_axis=2, tiled=True)  9.23 us
    all_to_all x1, waiting for transfers between devices, body(): lax.all_to_all(z_term, 'col', split_axis=2, concat_axis=1, tiled=True)  7.71 us
    all_to_all x1, starting transfers between devices, body(): lax.all_to_all(z_term, 'col', split_axis=2, concat_axis=1, tiled=True)  7.68 us
  transfers between devices with their start and end apart: 4, of which 3 were waited for; matrix products, arithmetic and copies ran while one was open for 13% of the time, Pallas kernels for 0%

commit v1 on v0

--- a/solution.py
+++ b/solution.py
@@ -5,6 +5,13 @@
 
 diffusion_coefficient = 0.5
 step_weight = 0.5
+
+
+def swap_blocks(shard, axis, split, join):
+    size = lax.axis_size(axis)
+    blocks = jnp.stack(jnp.split(shard, size, axis=split), axis=0)
+    blocks = lax.all_to_all(blocks, axis, split_axis=0, concat_axis=0)
+    return jnp.concatenate(blocks, axis=join)
 
 
 def contract_last(scalar_values, matrix):
@@ -62,7 +69,7 @@
     outgoing = jnp.transpose(outgoing, (0, 1, 3, 2)).reshape(
         scalar_count + 2, rows_local, length_x * depth_z
     )
-    pencil_y = lax.all_to_all(outgoing, "row", split_axis=2, concat_axis=1, tiled=True)
+    pencil_y = swap_blocks(outgoing, "row", 2, 1)
     y_term = axis_contribution(
         pencil_y[:scalar_count], pencil_y[scalar_count], first_y, second_y, contract_middle
     )

time: 202 us -> 194 us (0.960)
  local copies, waits for them, and re-layouts: 65 us -> 58.5 us
    reshape x1 -> x0, local copies, waits for them, and re-layouts: 6.77 us -> none  [body(): jnp.transpose(outgoing, (0, 1, 3, 2))]
    another operation x0 -> x16, local copies, waits for them, and re-layouts: none -> 4.8 us  [swap_blocks(): blocks = jnp.stack(jnp.split(shard, size, axis=split), axis=0)]
    all_to_all x1, local copies, waits for them, and re-layouts: 4.22 us -> 0.03 us  [swap_blocks(): blocks = lax.all_to_all(blocks, axis, split_axis=0, concat_axis=0)]
    split x0 -> x2, local copies, waits for them, and re-layouts: none -> 3.05 us  [swap_blocks(): blocks = jnp.stack(jnp.split(shard, size, axis=split), axis=0)]
    unnamed x21 -> x38, local copies, waits for them, and re-layouts: 25.8 us -> 23.3 us
  transfers between devices with their start and end apart: 4 -> 4, of which waited for: 3 -> 4; matrix products, arithmetic and copies ran while one was open for 13% -> 13% of each run, Pallas kernels for 0% -> 0%
where the time goes in v1:
time: 194 us
  local copies, waits for them, and re-layouts  58.5 us (30%)
  other arithmetic  40.8 us (21%)
  blocking collectives  33.8 us (17%)
  waiting for transfers between devices  26.7 us (14%)
  starting transfers between devices  26.5 us (14%)
  matrix products  6.88 us (4%)
    unnamed x1, other arithmetic  38.4 us
    all_to_all x1, blocking collectives, swap_blocks(): blocks = lax.all_to_all(blocks, axis, split_axis=0, concat_axis=0)  33.8 us
    unnamed x38, local copies, waits for them, and re-layouts  23.3 us
    all_to_all x1, waiting for transfers between devices, body(): lax.all_to_all(z_lines, 'row', split_axis=1, concat_axis=2, tiled=True)  15.7 us
    all_to_all x1, starting transfers between devices, body(): lax.all_to_all(z_lines, 'row', split_axis=1, concat_axis=2, tiled=True)  9.07 us
    reshape x4, local copies, waits for them, and re-layouts, contract_z(): matrix.reshape(matrix.shape[0] // depth_z, depth_z, blocks, depth_z)  8.7 us
    all_to_all x1, waiting for transfers between devices, body(): lax.all_to_all(z_term, 'col', split_axis=2, concat_axis=1, tiled=True)  7.71 us
    all_to_all x1, starting transfers between devices, body(): lax.all_to_all(z_term, 'col', split_axis=2, concat_axis=1, tiled=True)  7.34 us
  transfers between devices with their start and end apart: 4, of which 4 were waited for; matrix products, arithmetic and copies ran while one was open for 13% of the time, Pallas kernels for 0%

profile of v1, /device:TPU:8, one launch (start us, length us, event | category | flops | bytes accessed | tf_op | source)
XLA Modules:
  0.0 193.6 jit_solution(3957221521961476747)
XLA Ops:
  0.0 1.0 convert_element_type.74
  1.0 1.0 slice.32
  2.1 3.4 %copy.51 = bf16[3,16,512,8]{1,3,2,0:T(8,128)(2,1)} copy(bf16[3,16,512,8]{2,3,1,0:T(8,128)(2,1)S(1)} %maximum_bitcast_fusion) | data formatting | bytes 786432 | tf_op jit(solution)/shard_map/transpose | solution.py:69
  5.5 2.9 %fusion.33 = (bf16[3,16,256]{1,2,0:T(8,128)(2,1)S(1)}, bf16[1,3,16,256]{2,3,1,0:T(8,128)(2,1)S(1)}, bf16[1,3,16,256]{2,3,1,0:T(8,128)(2,1)S(1)}, bf16[1,3,16,256...) fusion(bf16[3,16,4096]{1,2,0:T(8,128)(2,1)} %bitcast.172), kind=kLoop, calls=%fused_computation.84 | loop fusion | bytes 786432 | tf_op jit(solution)/shard_map/split | solution.py:12
  8.4 1.0 copy.53
  10.1 1.0 copy.54
  14.0 1.3 constant_dynamic-update-slice_fusion.13
  23.2 33.8 %all_to_all.56 = bf16[16,3,16,256]{3,2,1,0:T(8,128)(2,1)S(1)} all-to-all(bf16[16,3,16,256]{3,2,1,0:T(8,128)(2,1)} %constant_dynamic-update-slice_fusion), channel_id=1, replica_groups=mesh['row'=16,'col'=32] {'row'}, dimensions={0} | all-to-all | bytes 786432 | tf_op jit(solution)/shard_map/all_to_all | solution.py:13
  57.1 1.0 copy.71
  58.1 5.9 %all-to-all-start.2 = ((bf16[2,256,256]{2,0,1:T(2,128)(2,1)}), bf16[2,256,256]{2,0,1:T(2,128)(2,1)S(1)}, u32[]{:S(2)}, u32[]{:S(2)}) async-start(bf16[2,256,256]{2,0,1:T(2,128)(2,1)} %copy.71), calls=%async_computation.2 | async-start | bytes 524288 | tf_op jit(solution)/shard_map/all_to_all | solution.py:77
  64.1 2.5 %reshape.135 = bf16[32,8,32,8]{3,2,1,0:T(8,128)(2,1)S(1)} reshape(bf16[256,256]{1,0:T(8,128)(2,1)S(1)} %copy-done.7) | data formatting | bytes 262144 | tf_op jit(solution)/shard_map/reshape | solution.py:33
  66.5 1.9 copy.76
  68.4 2.5 %reshape.136 = bf16[32,8,32,8]{3,2,1,0:T(8,128)(2,1)S(1)} reshape(bf16[256,256]{1,0:T(8,128)(2,1)S(1)} %copy-done.8) | data formatting | bytes 262144 | tf_op jit(solution)/shard_map/reshape | solution.py:33
  70.9 1.9 copy.82
  73.8 1.0 copy.74
  74.8 1.1 copy.78
  75.9 2.0 %fusion.1 = f32[1,8,32,32,8]{2,3,4,1,0:T(8,128)S(1)} fusion(bf16[32,8,32,8]{2,0,3,1:T(8,128)(2,1)} %copy.82, bf16[8,32,32,8,1]{1,3,2,0,4:T(8,128)(2,1)} %bitcast.186), kind=kOutput, calls=%fused_computation.2 | convolution fusion | flops 33619968 | bytes 524288 | tf_op jit(solution)/shard_map/sajxz,JZjz->saJxZ/dot_general | solution.py:34
  79.5 4.4 %copy.104 = f32[1,8,32,32,8]{1,4,3,2,0:T(8,128)} copy(f32[1,8,32,32,8]{2,3,4,1,0:T(8,128)S(1)} %fusion.4) | data formatting | bytes 524288 | tf_op jit(solution)/shard_map/reshape | solution.py:85
  84.4 38.4 %reduce = f32[8192,8]{1,0:T(8,128)} reduce(f32[8192,1,8]{2,1,0:T(1,128)} %bitcast.170, f32[]{:T(128)} %broadcast.21), dimensions={1}, to_apply=%bitcast.160.reduce_sub_computation | reduce | bytes 524292
  122.7 4.5 %reshape.152 = f32[32,1,2048]{2,1,0:T(1,128)} reshape(f32[8192,8]{1,0:T(8,128)} %reduce) | data formatting | bytes 524288
  127.3 7.3 %all-to-all-start.3 = ((f32[32,1,2048]{2,1,0:T(1,128)}), f32[32,1,2048]{2,1,0:T(1,128)S(1)}, u32[]{:S(2)}, u32[]{:S(2)}) async-start(f32[32,1,2048]{2,1,0:T(1,128)} %reshape.152), calls=%async_computation.3 | async-start | bytes 524288 | tf_op jit(solution)/shard_map/all_to_all | solution.py:86
  135.4 0.8 copy.70
  136.2 7.7 %all-to-all-done.3 = f32[32,1,2048]{2,1,0:T(1,128)S(1)} async-done(((f32[32,1,2048]{2,1,0:T(1,128)}), f32[32,1,2048]{2,1,0:T(1,128)S(1)}, u32[]{:S(2)}, u32[]{:S(2)}) %all-to-all-start.3) | async-done | bytes 262176 | tf_op jit(solution)/shard_map/all_to_all | solution.py:86
  143.9 4.2 %all-to-all-start.1 = ((f32[1,256,256]{2,0,1:T(1,128)}), f32[1,256,256]{2,0,1:T(1,128)S(1)}, u32[]{:S(2)}, u32[]{:S(2)}) async-start(f32[1,256,256]{2,0,1:T(1,128)} %copy.70), calls=%async_computation.1 | async-start | bytes 524288 | tf_op jit(solution)/shard_map/all_to_all | solution.py:88
  148.1 1.2 reduce.1
  149.3 8.4 %reshape.153 = f32[8192,1,8]{2,1,0:T(1,128)} reshape(f32[32,2048]{1,0:T(8,128)S(1)} %reduce.1) | data formatting | bytes 524288
  157.7 2.9 %copy.105 = f32[1,8,32,256]{3,2,1,0:T(8,128)S(1)} copy(f32[1,8,32,256]{1,3,2,0:T(8,128)} %bitcast.171) | data formatting | bytes 524288 | tf_op jit(solution)/shard_map/all_to_all | solution.py:86
  160.8 1.0 copy.87
  161.7 3.0 %all-to-all-done.1 = f32[1,256,256]{2,0,1:T(1,128)S(1)} async-done(((f32[1,256,256]{2,0,1:T(1,128)}), f32[1,256,256]{2,0,1:T(1,128)S(1)}, u32[]{:S(2)}, u32[]{:S(2)}) %all-to-all-start.1) | async-done | bytes 262176 | tf_op jit(solution)/shard_map/all_to_all | solution.py:88
  164.7 9.1 %all-to-all-start.4 = ((f32[1,256,256]{2,0,1:T(1,128)}), f32[1,256,256]{2,0,1:T(1,128)S(1)}, u32[]{:S(2)}, u32[]{:S(2)}) async-start(f32[1,256,256]{2,0,1:T(1,128)} %copy.87), calls=%async_computation.4 | async-start | bytes 524288 | tf_op jit(solution)/shard_map/all_to_all | solution.py:89
  174.4 15.7 %all-to-all-done.4 = f32[1,256,256]{2,0,1:T(1,128)S(1)} async-done(((f32[1,256,256]{2,0,1:T(1,128)}), f32[1,256,256]{2,0,1:T(1,128)S(1)}, u32[]{:S(2)}, u32[]{:S(2)}) %all-to-all-start.4) | async-done | bytes 262176 | tf_op jit(solution)/shard_map/all_to_all | solution.py:89
  191.6 2.1 %fusion.17 = f32[1,16,8,512]{3,2,1,0:T(8,128)} fusion(f32[1,16,8,512]{3,2,1,0:T(8,128)S(1)} %copy-done.1, f32[16,8,512]{2,1,0:T(8,128)S(1)} %fusion.9, bf16[512,512]{1,0:T(8,128)(2,1)} %param.11, f32[1,16,512,8]{2,3,1,0:T(8,128)S(1)} %copy.91, bf16[1,16,8,512]{3,2,1,0:T(8,128)(2,1)S(1)} %convert_element_type.74), kind=kOutput, calls=%fused_computation.26 | convolution fusion | flops 67436544 | bytes 1703936 | tf_op jit(solution)/shard_map/dot_general | solution.py:18
  (72 shorter events, 17.4 us)
Async XLA Ops:
  0.0 173.8 %copy-start = (bf16[512,512]{1,0:T(8,128)(2,1)S(1)}, bf16[512,512]{1,0:T(8,128)(2,1)}, u32[]{:S(2)}) copy-start(bf16[512,512]{1,0:T(8,128)(2,1)} %param.10) | copy-start | bytes 1572868
  12.5 51.5 %copy-start.7 = (bf16[256,256]{1,0:T(8,128)(2,1)S(1)}, bf16[256,256]{1,0:T(8,128)(2,1)}, u32[]{:S(2)}) copy-start(bf16[256,256]{1,0:T(8,128)(2,1)} %param.14) | copy-start | bytes 393220
  57.1 11.3 %copy-start.8 = (bf16[256,256]{1,0:T(8,128)(2,1)S(1)}, bf16[256,256]{1,0:T(8,128)(2,1)}, u32[]{:S(2)}) copy-start(bf16[256,256]{1,0:T(8,128)(2,1)} %param.15) | copy-start | bytes 393220
  58.1 15.2 %all-to-all-start.2 = ((bf16[2,256,256]{2,0,1:T(2,128)(2,1)}), bf16[2,256,256]{2,0,1:T(2,128)(2,1)S(1)}, u32[]{:S(2)}, u32[]{:S(2)}) async-start(bf16[2,256,256]{2,0,1:T(2,128)(2,1)} %copy.71), calls=%async_computation.2 | async-start | bytes 524288 | tf_op jit(solution)/shard_map/all_to_all | solution.py:77
  73.4 4.5 %copy-start.3 = (bf16[32,8,32,8]{2,0,3,1:T(8,128)(2,1)S(1)}, bf16[32,8,32,8]{2,0,3,1:T(8,128)(2,1)}, u32[]{:S(2)}) copy-start(bf16[32,8,32,8]{2,0,3,1:T(8,128)(2,1)} %copy.76) | copy-start | bytes 393220
  75.9 2.0 %copy-start.5 = (bf16[1,8,32,256]{2,3,1,0:T(8,128)(2,1)S(1)}, bf16[1,8,32,256]{2,3,1,0:T(8,128)(2,1)}, u32[]{:S(2)}) copy-start(bf16[1,8,32,256]{2,3,1,0:T(8,128)(2,1)} %copy.74) | copy-start | bytes 393220
  75.9 2.8 %copy-start.4 = (bf16[1,8,32,256]{2,3,1,0:T(8,128)(2,1)S(1)}, bf16[1,8,32,256]{2,3,1,0:T(8,128)(2,1)}, u32[]{:S(2)}) copy-start(bf16[1,8,32,256]{2,3,1,0:T(8,128)(2,1)} %copy.78) | copy-start | bytes 393220
  122.7 11.9 %copy-start.6 = (bf16[256,256]{1,0:T(8,128)(2,1)S(1)}, bf16[256,256]{1,0:T(8,128)(2,1)}, u32[]{:S(2)}) copy-start(bf16[256,256]{1,0:T(8,128)(2,1)} %param.12) | copy-start | bytes 393220
  122.7 12.4 %copy-start.9 = (bf16[256,256]{1,0:T(8,128)(2,1)S(1)}, bf16[256,256]{1,0:T(8,128)(2,1)}, u32[]{:S(2)}) copy-start(bf16[256,256]{1,0:T(8,128)(2,1)} %param.13) | copy-start | bytes 393220
  127.3 16.6 %all-to-all-start.3 = ((f32[32,1,2048]{2,1,0:T(1,128)}), f32[32,1,2048]{2,1,0:T(1,128)S(1)}, u32[]{:S(2)}, u32[]{:S(2)}) async-start(f32[32,1,2048]{2,1,0:T(1,128)} %reshape.152), calls=%async_computation.3 | async-start | bytes 524288 | tf_op jit(solution)/shard_map/all_to_all | solution.py:86
  143.9 20.8 %all-to-all-start.1 = ((f32[1,256,256]{2,0,1:T(1,128)}), f32[1,256,256]{2,0,1:T(1,128)S(1)}, u32[]{:S(2)}, u32[]{:S(2)}) async-start(f32[1,256,256]{2,0,1:T(1,128)} %copy.70), calls=%async_computation.1 | async-start | bytes 524288 | tf_op jit(solution)/shard_map/all_to_all | solution.py:88
  157.7 16.1 %copy-start.2 = (bf16[3,16,8,512]{3,2,1,0:T(8,128)(2,1)S(1)}, bf16[3,16,8,512]{3,2,1,0:T(8,128)(2,1)}, u32[]{:S(2)}) copy-start(bf16[3,16,8,512]{3,2,1,0:T(8,128)(2,1)} %param.9) | copy-start | bytes 1179652
  164.7 25.5 %all-to-all-start.4 = ((f32[1,256,256]{2,0,1:T(1,128)}), f32[1,256,256]{2,0,1:T(1,128)S(1)}, u32[]{:S(2)}, u32[]{:S(2)}) async-start(f32[1,256,256]{2,0,1:T(1,128)} %copy.87), calls=%async_computation.4 | async-start | bytes 524288 | tf_op jit(solution)/shard_map/all_to_all | solution.py:89
  174.1 17.5 %copy-start.1 = (f32[1,16,8,512]{3,2,1,0:T(8,128)S(1)}, f32[1,16,8,512]{3,2,1,0:T(8,128)}, u32[]{:S(2)}) copy-start(f32[1,16,8,512]{3,2,1,0:T(8,128)} %param.8) | copy-start | bytes 786436
